TPU v7x, 256 devices: a whole 4x4x8 slice. The times are simulated.
256 devices in a mesh: dp: 4 (over y), expert: 64 (over z, x, core).
Axes of the slice: x: 4, y: 4, z: 8, core: 2. Of those that a mesh axis runs over, the one named last changes fastest.
Arguments:
- tokens: bfloat16 [32768, 2048], P(('dp', 'expert')), may hold values from -6 to 6
- cotangent: bfloat16 [32768, 2048], P(('dp', 'expert')), may hold values from -3 to 3
- routes: int32 [32768, 1], P(('dp', 'expert')), may hold values from 0 to 63, as said below
- gate_fixed: int32 [32768, 1], P(('dp', 'expert')), may hold values from 8192 to 65535
- w_gate: bfloat16 [64, 2048, 768], P('expert', 'dp'), may hold values from -0.125 to 0.125
- w_up: bfloat16 [64, 2048, 768], P('expert', 'dp'), may hold values from -0.125 to 0.125
- w_down: bfloat16 [64, 768, 2048], P('expert', None, 'dp'), may hold values from -0.21875 to 0.21875
Outputs:
- mixed: bfloat16 [32768, 2048], P(('dp', 'expert'))
- grad_tokens: bfloat16 [32768, 2048], P(('dp', 'expert'))
- grad_w_gate: bfloat16 [64, 2048, 768], P('expert', 'dp')
- grad_w_up: bfloat16 [64, 2048, 768], P('expert', 'dp')
- grad_w_down: bfloat16 [64, 768, 2048], P('expert', None, 'dp')
Inputs may be any that keep to these rules, and one draw needn't show every extreme that they name: `routes`: each token names one expert. Among the tokens of one device no expert is named more than 3 times, and some experts are named exactly 3 times by the tokens of every device.
All inputs are finite; a program needn't handle non-finite values.
Results may differ from a plain program's by a relative error of at most 0.0058.
Values may be sent and summed in bfloat16 or wider, within the bound.
A program may use at most 64 MiB of HBM per device.

v0:
```python
import jax
import jax.numpy as jnp
from jax import lax
from jax.sharding import Mesh
from jax.sharding import PartitionSpec as P

EXPERT = ("expert_0", "expert_1", "expert_2")
DP_EXPERT = ("dp", "expert_0", "expert_1", "expert_2")


def in_blocks(array, dim, size):
    lengths = array.shape
    tiles = array.reshape(*lengths[:dim], size, lengths[dim] // size, *lengths[dim + 1 :])
    return jnp.moveaxis(tiles, dim, 0)


def joined_along(tiles, dim):
    tiles = jnp.moveaxis(tiles, 0, dim)
    lengths = tiles.shape
    return tiles.reshape(*lengths[:dim], lengths[dim] * lengths[dim + 1], *lengths[dim + 2 :])


def turned_blocks(tiles, axes, turns):
    lengths = [lax.axis_size(a) for a in axes]
    tiles = tiles.reshape(*lengths, *tiles.shape[1:])
    for k in turns:
        tiles = lax.all_to_all(tiles, axes[k], split_axis=k, concat_axis=k, tiled=True)
    return tiles.reshape(-1, *tiles.shape[len(axes) :])


def two_step_exchange(array, groups, turns, split_dim, concat_dim):
    size = lax.axis_size(groups[0]) * lax.axis_size(groups[1])
    tiles = in_blocks(array, split_dim, size)
    return joined_along(turned_blocks(tiles, groups, turns), concat_dim)


def gather_turned(arrays, axis, dims):
    turned = [jnp.moveaxis(a, dim, 0) for a, dim in zip(arrays, dims)]
    widths = [t[0].size for t in turned]
    both = jnp.concatenate([t.reshape(-1, w) for t, w in zip(turned, widths)], axis=1)
    filled = lax.all_gather(both, axis, axis=0, tiled=True)
    tiles = jnp.split(filled, [sum(widths[:k]) for k in range(1, len(widths))], axis=1)
    return tuple(
        (
            jnp.moveaxis(b.reshape(-1, *t.shape[1:]), 0, dim)
            for b, t, dim in zip(tiles, turned, dims)
        )
    )


def sent_together(arrays, axis, split_dim, concat_dim, along):
    ends, at = ([], 0)
    for a in arrays[:-1]:
        at += a.shape[along]
        ends.append(at)
    both = jnp.concatenate(arrays, axis=along)
    return tuple(
        jnp.split(
            lax.all_to_all(both, axis, split_axis=split_dim, concat_axis=concat_dim, tiled=True),
            ends,
            axis=along,
        )
    )


def in_one_piece(arrays, axis, dim, along):
    both = jnp.concatenate(arrays, axis=along)
    filled, at, gathered = (lax.all_gather(both, axis, axis=dim, tiled=True), 0, [])
    for a in arrays:
        gathered.append(lax.slice_in_dim(filled, at, at + a.shape[along], axis=along))
        at += a.shape[along]
    return tuple(gathered)


def swap_experts(buffer):
    return two_step_exchange(buffer, (("expert_0", "expert_1"), "expert_2"), (0, 1), 1, 1)


def contract_last(left_side, right_side):
    return lax.dot_general(
        left_side, right_side, (((1,), (1,)), ((), ())), preferred_element_type=jnp.float32
    )


def contract_first(left_side, right_side):
    return lax.dot_general(
        left_side, right_side, (((0,), (0,)), ((), ())), preferred_element_type=jnp.float32
    )


def gate_gradients(grad_hidden, gate_pre, up_pre):
    sigmoid_gate = jax.nn.sigmoid(gate_pre)
    grad_gate = grad_hidden * up_pre * sigmoid_gate * (1.0 + gate_pre * (1.0 - sigmoid_gate))
    grad_up = grad_hidden * gate_pre * sigmoid_gate
    return jnp.concatenate([grad_gate, grad_up], axis=1).astype(jnp.bfloat16)


def full_width_pass(outgoing, grad_outgoing, gate_up_w, down_all, shape_out):
    expert_count, capacity, model_width = shape_out
    own_rows = expert_count * capacity
    hidden_width = down_all.shape[0]
    received = swap_experts(outgoing)
    flat_received = received.reshape(own_rows, model_width)
    gate_up = jnp.dot(flat_received, gate_up_w, preferred_element_type=jnp.float32)
    gate_pre = gate_up[:, :hidden_width]
    up_pre = gate_up[:, hidden_width:]
    hidden = (gate_pre * jax.nn.sigmoid(gate_pre) * up_pre).astype(jnp.bfloat16)
    slot_out = jnp.dot(hidden, down_all, preferred_element_type=jnp.float32).astype(jnp.bfloat16)
    returned = swap_experts(slot_out.reshape(1, expert_count, capacity, model_width)).reshape(
        own_rows, model_width
    )
    grad_received = swap_experts(grad_outgoing)
    grad_hidden = contract_last(grad_received.reshape(own_rows, model_width), down_all)
    grad_gate_up = gate_gradients(grad_hidden, gate_pre, up_pre)
    slot_grad_in = contract_last(grad_gate_up, gate_up_w).astype(jnp.bfloat16)
    grad_returned = swap_experts(
        slot_grad_in.reshape(1, expert_count, capacity, model_width)
    ).reshape(own_rows, model_width)
    return (received, grad_received, hidden, grad_gate_up, returned, grad_returned)


def body(tokens, cotangent, routes, gate_fixed, w_gate, w_up, w_down):
    tok_count = tokens.shape[0]
    model_width = tokens.shape[1]
    route_count = routes.shape[1]
    hidden_width = w_gate.shape[2]
    expert_count = lax.axis_size(EXPERT)
    capacity = 3 * tok_count * route_count // (2 * expert_count)
    own_rows = expert_count * capacity
    flat_total = tok_count * route_count
    route_weight = gate_fixed.astype(jnp.float32) / 65536.0
    flat_routes = routes.reshape(flat_total)
    one_hot = (flat_routes[:, None] == jnp.arange(expert_count, dtype=jnp.int32)[None, :]).astype(
        jnp.int32
    )
    position = jnp.sum((jnp.cumsum(one_hot, axis=0) - one_hot) * one_hot, axis=1)
    slot_index = flat_routes * capacity + position
    matches = slot_index[None, :] == jnp.arange(own_rows, dtype=jnp.int32)[:, None]
    occupied = jnp.any(matches, axis=1)
    source_row = jnp.sum(
        jnp.where(matches, jnp.arange(flat_total, dtype=jnp.int32)[None, :], 0), axis=1
    )
    slot_weight = jnp.sum(
        jnp.where(matches, route_weight.reshape(flat_total)[None, :], 0.0), axis=1
    )
    token_row = source_row // route_count
    outgoing = jnp.where(
        occupied[:, None], jnp.take(tokens, token_row, axis=0), jnp.zeros((), tokens.dtype)
    )
    outgoing = outgoing.reshape(1, expert_count, capacity, model_width)
    scaled = (
        slot_weight[:, None] * jnp.take(cotangent, token_row, axis=0).astype(jnp.float32)
    ).astype(jnp.bfloat16)
    grad_outgoing = jnp.where(occupied[:, None], scaled, jnp.zeros((), scaled.dtype))
    grad_outgoing = grad_outgoing.reshape(1, expert_count, capacity, model_width)
    shape_out = (expert_count, capacity, model_width)
    replicas = lax.axis_size("dp")
    part_width = model_width // replicas
    gate_all, up_all, down_all = gather_turned((w_gate[0], w_up[0], w_down[0]), "dp", (0, 0, 1))
    gate_up_w = jnp.concatenate([gate_all, up_all], axis=1)
    received, grad_received, hidden, grad_gate_up, returned, grad_returned = full_width_pass(
        outgoing, grad_outgoing, gate_up_w, down_all, shape_out
    )
    slot_cols, grad_cols = sent_together((received, grad_received), "dp", 3, 0, 1)
    hidden_all, grad_gate_up_all = in_one_piece((hidden, grad_gate_up), "dp", 0, 1)
    slot_cols = slot_cols.reshape(replicas * own_rows, part_width)
    grad_cols = grad_cols.reshape(replicas * own_rows, part_width)
    gate_up_grad = contract_first(slot_cols, grad_gate_up_all)
    down_grad = contract_first(hidden_all, grad_cols)
    picked = (
        jnp.take(returned, slot_index, axis=0)
        .reshape(tok_count, route_count, model_width)
        .astype(jnp.float32)
    )
    mixed = jnp.sum(route_weight[:, :, None] * picked, axis=1).astype(jnp.bfloat16)
    grad_picked = (
        jnp.take(grad_returned, slot_index, axis=0)
        .reshape(tok_count, route_count, model_width)
        .astype(jnp.float32)
    )
    grad_tokens = jnp.sum(grad_picked, axis=1).astype(jnp.bfloat16)
    grad_w_gate = gate_up_grad[:, :hidden_width].astype(jnp.bfloat16)[None]
    grad_w_up = gate_up_grad[:, hidden_width:].astype(jnp.bfloat16)[None]
    grad_w_down = down_grad.astype(jnp.bfloat16)[None]
    return (mixed, grad_tokens, grad_w_gate, grad_w_up, grad_w_down)


def solution(mesh):
    finer = Mesh(
        mesh.devices.reshape(mesh.shape["dp"], 8, 4, 2), ("dp", "expert_0", "expert_1", "expert_2")
    )
    placed = (
        P(DP_EXPERT, None),
        P(DP_EXPERT, None),
        P(DP_EXPERT, None),
        P(DP_EXPERT, None),
        P(EXPERT, "dp", None),
        P(EXPERT, "dp", None),
        P(EXPERT, None, "dp"),
    )
    return jax.shard_map(
        body,
        mesh=finer,
        in_specs=placed,
        out_specs=(
            P(DP_EXPERT, None),
            P(DP_EXPERT, None),
            P(EXPERT, "dp", None),
            P(EXPERT, "dp", None),
            P(EXPERT, None, "dp"),
        ),
        check_vma=False,
    )
```

profile of v0, /device:TPU:1, one launch (start us, length us, event | category | flops | bytes accessed | tf_op | source)
XLA Modules:
  0.0 254.6 jit_solution(7288200320655958101)
XLA Ops:
  7.2 1.5 copy.61
  8.7 1.4 copy.60
  10.2 1.6 pad_maximum_fusion
  11.7 0.6 copy-done.8
  13.0 2.0 gather_fusion.2
  15.0 2.0 gather_fusion
  17.3 1.7 fusion.17
  19.1 0.5 reshape_transpose_reshape_reshape.12
  19.6 1.9 copy.57
  21.4 11.9 %all-to-all-start = ((bf16[32,2,1,1,3,2048]{5,1,4,3,2,0:T(2,128)(2,1)}), bf16[32,2,1,1,3,2048]{5,1,4,3,2,0:T(2,128)(2,1)S(1)}, u32[]{:S(2)}, u32[]{:S(2)}) async-start(bf16[32,2,1,1,3,2048]{5,1,4,3,2,0:T(2,128)(2,1)} %copy.57), calls=%async_computation | async-start | bytes 1572864 | tf_op jit(solution)/shard_map/all_to_all | solution.py:27
  33.3 0.5 reshape_transpose_reshape_reshape.14
  33.8 1.9 copy.65
  35.7 18.7 %all-to-all-done = bf16[32,2,1,1,3,2048]{5,1,4,3,2,0:T(2,128)(2,1)S(1)} async-done(((bf16[32,2,1,1,3,2048]{5,1,4,3,2,0:T(2,128)(2,1)}), bf16[32,2,1,1,3,2048]{5,1,4,3,2,0:T(2,128)(2,1)S(1)}, u32[]{:S(2)}, u32[]{:S(2)}) %all-to-all-start) | async-done | bytes 786464 | tf_op jit(solution)/shard_map/all_to_all | solution.py:27
  54.6 6.8 %all_to_all.58 = bf16[32,2,1,1,3,2048]{5,0,4,3,2,1:T(8,128)(2,1)S(1)} all-to-all(bf16[32,2,1,1,3,2048]{5,0,4,3,2,1:T(8,128)(2,1)S(1)} %copy.58), channel_id=1, replica_groups=mesh['dp'=4,'expert_0'=8,'expert_1'=4,'expert_2'=2] {'expert_2'}, dimensions={1} | all-to-all | bytes 1572864 | tf_op jit(solution)/shard_map/all_to_all | solution.py:27
  61.4 4.8 %all-to-all-start.4 = ((bf16[32,2,1,1,3,2048]{5,1,4,3,2,0:T(2,128)(2,1)}), bf16[32,2,1,1,3,2048]{5,1,4,3,2,0:T(2,128)(2,1)S(1)}, u32[]{:S(2)}, u32[]{:S(2)}) async-start(bf16[32,2,1,1,3,2048]{5,1,4,3,2,0:T(2,128)(2,1)} %copy.65), calls=%async_computation.4 | async-start | bytes 1572864 | tf_op jit(solution)/shard_map/all_to_all | solution.py:27
  66.3 0.7 copy.59
  67.0 1.4 reshape_reshape_transpose_reshape.12
  68.4 19.1 %all-to-all-done.4 = bf16[32,2,1,1,3,2048]{5,1,4,3,2,0:T(2,128)(2,1)S(1)} async-done(((bf16[32,2,1,1,3,2048]{5,1,4,3,2,0:T(2,128)(2,1)}), bf16[32,2,1,1,3,2048]{5,1,4,3,2,0:T(2,128)(2,1)S(1)}, u32[]{:S(2)}, u32[]{:S(2)}) %all-to-all-start.4) | async-done | bytes 786464 | tf_op jit(solution)/shard_map/all_to_all | solution.py:27
  87.8 6.8 %all_to_all.59 = bf16[32,2,1,1,3,2048]{5,0,4,3,2,1:T(8,128)(2,1)S(1)} all-to-all(bf16[32,2,1,1,3,2048]{5,0,4,3,2,1:T(8,128)(2,1)S(1)} %copy.66), channel_id=1, replica_groups=mesh['dp'=4,'expert_0'=8,'expert_1'=4,'expert_2'=2] {'expert_2'}, dimensions={1} | all-to-all | bytes 1572864 | tf_op jit(solution)/shard_map/all_to_all | solution.py:27
  94.6 0.7 copy.67
  95.3 1.4 reshape_reshape_transpose_reshape.14
  96.7 13.3 %all-gather.3.cloned.1.call-done = bf16[2048,2304]{0,1:T(8,128)(2,1)} async-done(((bf16[512,2304]{0,1:T(8,128)(2,1)}), bf16[2048,2304]{0,1:T(8,128)(2,1)}) %all-gather.3.cloned.1.call-update) | async-done | bytes 9437200 | tf_op jit(solution)/shard_map/all_gather | solution.py:41
  110.0 5.3 %fusion.2 = f32[192,1536]{1,0:T(8,128)S(1)} fusion(bf16[192,2048]{1,0:T(8,128)(2,1)} %reshape_reshape_transpose_reshape.12, bf16[2048,2304]{0,1:T(8,128)(2,1)} %all-gather.3.cloned.1.call-done), kind=kOutput, calls=%fused_computation.6 | convolution fusion | flops 1207959552 | bytes 8257536 | tf_op jit(solution)/shard_map/dot_general | solution.py:104
  115.3 3.3 %multiply_convert_fusion.3 = (bf16[192,768]{1,0:T(8,128)(2,1)S(1)}, bf16[192,768]{1,0:T(8,128)(2,1)S(1)}, bf16[192,768]{1,0:T(8,128)(2,1)S(1)}) fusion(f32[192,1536]{1,0:T(8,128)S(1)} %fusion.2, bf16[192,2048]{1,0:T(8,128)(2,1)S(1)} %copy-done.6, bf16[2048,2304]{0,1:T(8,128)(2,1)} %all-gather.3.cloned.1.call-done), kind=kOutput, calls=%fused_computation.32 | convolution fusion | flops 606339072 | bytes 5996544 | tf_op jit(solution)/shard_map/dot_general | solution.py:80
  118.6 0.7 copy-done.7
  119.3 1.0 pad_maximum_fusion.2
  120.3 3.6 %fusion.8 = bf16[192,2048]{1,0:T(8,128)(2,1)} fusion(bf16[192,768]{1,0:T(8,128)(2,1)S(1)} %get-tuple-element.15, bf16[2048,2304]{0,1:T(8,128)(2,1)} %all-gather.3.cloned.1.call-done), kind=kOutput, calls=%fused_computation.13 | convolution fusion | flops 604372992 | bytes 4227072 | tf_op jit(solution)/shard_map/dot_general | solution.py:108
  123.8 2.4 reshape_transpose_reshape_reshape.13
  126.3 1.9 copy.62
  128.2 9.5 %all-to-all-start.2 = ((bf16[32,2,1,1,3,2048]{5,1,4,3,2,0:T(2,128)(2,1)}), bf16[32,2,1,1,3,2048]{5,1,4,3,2,0:T(2,128)(2,1)S(1)}, u32[]{:S(2)}, u32[]{:S(2)}) async-start(bf16[32,2,1,1,3,2048]{5,1,4,3,2,0:T(2,128)(2,1)} %copy.62), calls=%async_computation.2 | async-start | bytes 1572864 | tf_op jit(solution)/shard_map/all_to_all | solution.py:27
  137.7 1.7 copy.72
  139.4 3.0 %reshape_transpose_reshape.7 = bf16[1,64,3,2048]{3,1,2,0:T(8,128)(2,1)} reshape(bf16[32,2,1,1,3,2048]{5,1,0,4,3,2:T(2,128)(2,1)} %copy.72) | data formatting | bytes 1572864 | tf_op jit(solution)/shard_map/reshape;transpose;reshape | solution.py:20
  142.3 0.8 copy.71
  143.2 1.2 reshape_transpose_reshape.6
  144.3 1.5 pad_maximum_fusion.1
  145.8 2.6 %copy.73 = bf16[1,128,3,2048]{1,2,0,3:T(4,128)(2,1)} copy(bf16[1,128,3,2048]{3,1,2,0:T(8,128)(2,1)S(1)} %pad_maximum_fusion.1) | data formatting | bytes 3145728 | tf_op jit(solution)/shard_map/concatenate | solution.py:56
  148.4 10.4 %all-to-all-done.2 = bf16[32,2,1,1,3,2048]{5,1,4,3,2,0:T(2,128)(2,1)S(1)} async-done(((bf16[32,2,1,1,3,2048]{5,1,4,3,2,0:T(2,128)(2,1)}), bf16[32,2,1,1,3,2048]{5,1,4,3,2,0:T(2,128)(2,1)S(1)}, u32[]{:S(2)}, u32[]{:S(2)}) %all-to-all-start.2) | async-done | bytes 786464 | tf_op jit(solution)/shard_map/all_to_all | solution.py:27
  158.7 3.8 %all-to-all-start.8 = ((bf16[1,128,3,2048]{1,2,0,3:T(4,128)(2,1)}), bf16[1,128,3,2048]{1,2,0,3:T(4,128)(2,1)S(1)}, u32[]{:S(2)}, u32[]{:S(2)}) async-start(bf16[1,128,3,2048]{1,2,0,3:T(4,128)(2,1)} %copy.73), calls=%async_computation.8 | async-start | bytes 4194304 | tf_op jit(solution)/shard_map/all_to_all | solution.py:59
  162.6 5.2 %fusion.11 = bf16[192,2048]{1,0:T(8,128)(2,1)} fusion(bf16[2048,2304]{0,1:T(8,128)(2,1)} %all-gather.3.cloned.1.call-done, bf16[192,768]{1,0:T(8,128)(2,1)} %copy-done.7, bf16[192,768]{1,0:T(8,128)(2,1)S(1)} %get-tuple-element.9), kind=kOutput, calls=%fused_computation.14 | convolution fusion | flops 1209532416 | bytes 7667712 | tf_op jit(solution)/shard_map/dot_general | solution.py:80
  167.8 3.3 %reshape_transpose_reshape_reshape.15 = bf16[32,2,1,1,3,2048]{5,4,1,0,3,2:T(4,128)(2,1)} reshape(bf16[192,2048]{1,0:T(8,128)(2,1)} %fusion.11) | data formatting | bytes 1572864 | tf_op jit(solution)/shard_map/reshape;transpose;reshape;reshape | solution.py:25
  171.0 3.1 %copy.68 = bf16[32,2,1,1,3,2048]{5,1,4,3,2,0:T(2,128)(2,1)} copy(bf16[32,2,1,1,3,2048]{5,4,1,0,3,2:T(4,128)(2,1)} %reshape_transpose_reshape_reshape.15) | data formatting | bytes 1572864 | tf_op jit(solution)/shard_map/reshape;transpose;reshape;reshape | solution.py:25
  174.1 1.1 copy.63
  175.3 10.9 %all-to-all-done.8 = bf16[1,128,3,2048]{1,2,0,3:T(4,128)(2,1)S(1)} async-done(((bf16[1,128,3,2048]{1,2,0,3:T(4,128)(2,1)}), bf16[1,128,3,2048]{1,2,0,3:T(4,128)(2,1)S(1)}, u32[]{:S(2)}, u32[]{:S(2)}) %all-to-all-start.8) | async-done | bytes 1572896 | tf_op jit(solution)/shard_map/all_to_all | solution.py:59
  186.1 9.8 %all_to_all.60 = bf16[32,2,1,1,3,2048]{5,0,4,3,2,1:T(8,128)(2,1)} all-to-all(bf16[32,2,1,1,3,2048]{5,0,4,3,2,1:T(8,128)(2,1)} %copy.63), channel_id=1, replica_groups=mesh['dp'=4,'expert_0'=8,'expert_1'=4,'expert_2'=2] {'expert_2'}, dimensions={1} | all-to-all | bytes 1572864 | tf_op jit(solution)/shard_map/all_to_all | solution.py:27
  196.0 9.6 %all-to-all-start.6 = ((bf16[32,2,1,1,3,2048]{5,1,4,3,2,0:T(2,128)(2,1)}), bf16[32,2,1,1,3,2048]{5,1,4,3,2,0:T(2,128)(2,1)}, u32[]{:S(2)}, u32[]{:S(2)}) async-start(bf16[32,2,1,1,3,2048]{5,1,4,3,2,0:T(2,128)(2,1)} %copy.68), calls=%async_computation.6 | async-start | bytes 1572864 | tf_op jit(solution)/shard_map/all_to_all | solution.py:27
  205.9 1.8 fusion.24
  207.7 2.8 %copy.75 = bf16[4,64,3,512]{3,2,1,0:T(4,128)(2,1)S(1)} copy(bf16[4,64,3,512]{1,3,0,2:T(8,128)(2,1)} %get-tuple-element.12) | data formatting | bytes 1572864 | tf_op jit(solution)/shard_map/split | solution.py:58
  210.5 1.4 reshape.53
  212.0 1.2 copy.76
  213.1 1.4 reshape.54
  214.6 1.8 copy.64
  216.4 0.7 reshape_reshape_transpose_reshape.13
  217.1 9.8 %all-to-all-done.6 = bf16[32,2,1,1,3,2048]{5,1,4,3,2,0:T(2,128)(2,1)} async-done(((bf16[32,2,1,1,3,2048]{5,1,4,3,2,0:T(2,128)(2,1)}), bf16[32,2,1,1,3,2048]{5,1,4,3,2,0:T(2,128)(2,1)}, u32[]{:S(2)}, u32[]{:S(2)}) %all-to-all-start.6) | async-done | bytes 786464 | tf_op jit(solution)/shard_map/all_to_all | solution.py:27
  226.9 1.4 copy.69
  228.3 6.7 %all_to_all.61 = bf16[32,2,1,1,3,2048]{5,0,4,3,2,1:T(8,128)(2,1)S(1)} all-to-all(bf16[32,2,1,1,3,2048]{5,0,4,3,2,1:T(8,128)(2,1)S(1)} %copy.69), channel_id=1, replica_groups=mesh['dp'=4,'expert_0'=8,'expert_1'=4,'expert_2'=2] {'expert_2'}, dimensions={1} | all-to-all | bytes 1572864 | tf_op jit(solution)/shard_map/all_to_all | solution.py:27
  235.0 0.7 copy.70
  235.7 0.7 reshape_reshape_transpose_reshape.15
  236.4 0.9 gather_fusion.1
  237.4 0.9 gather_fusion.3
  238.3 0.9 broadcast_select_fusion
  239.2 1.1 multiply_convert_fusion.1
  240.3 3.1 %convolution_convert_fusion = bf16[512,1536]{1,0:T(8,128)(2,1)S(1)} fusion(bf16[768,512]{1,0:T(8,128)(2,1)S(1)} %copy-done.5, bf16[768,2304]{1,0:T(8,128)(2,1)} %all-gather.5.cloned.1.call-done), kind=kOutput, calls=%fused_computation.8 | convolution fusion | flops 1208745984 | bytes 4718592 | tf_op jit(solution)/shard_map/dot_general | solution.py:86
  243.4 1.2 slice_bitcast_fusion
  244.8 3.0 %fusion.15 = bf16[1,768,512]{2,1,0:T(8,128)(2,1)} fusion(bf16[768,512]{1,0:T(8,128)(2,1)S(1)} %copy-done.4, bf16[768,2304]{1,0:T(8,128)(2,1)} %all-gather.5.cloned.1.call-done), kind=kOutput, calls=%fused_computation.20 | convolution fusion | flops 604372992 | bytes 2752512 | tf_op jit(solution)/shard_map/dot_general | solution.py:86
  (39 shorter events, 1.8 us)
Async XLA Ops:
  7.2 5.8 %copy-start = (bf16[128,2048]{1,0:T(8,128)(2,1)S(1)}, bf16[128,2048]{1,0:T(8,128)(2,1)}, u32[]{:S(2)}) copy-start(bf16[128,2048]{1,0:T(8,128)(2,1)} %param.12) | copy-start | bytes 1572868
  7.2 3.0 %copy-start.3 = (bf16[1,768,512]{2,1,0:T(8,128)(2,1)S(1)}, bf16[1,768,512]{2,1,0:T(8,128)(2,1)}, u32[]{:S(2)}) copy-start(bf16[1,768,512]{2,1,0:T(8,128)(2,1)} %param.17) | copy-start | bytes 2359300
  7.2 102.8 %all-gather.3.cloned.1.call-start = ((), (), s32[]{:S(2)}) async-start(), calls=%async_computation.9 | async-start | bytes 11796480 | tf_op jit(solution)/shard_map/all_gather | solution.py:41
  11.7 0.7 copy-start.8
  13.0 2.0 copy-start.2
  15.0 2.1 copy-start.9
  21.4 32.9 %all-to-all-start = ((bf16[32,2,1,1,3,2048]{5,1,4,3,2,0:T(2,128)(2,1)}), bf16[32,2,1,1,3,2048]{5,1,4,3,2,0:T(2,128)(2,1)S(1)}, u32[]{:S(2)}, u32[]{:S(2)}) async-start(bf16[32,2,1,1,3,2048]{5,1,4,3,2,0:T(2,128)(2,1)} %copy.57), calls=%async_computation | async-start | bytes 1572864 | tf_op jit(solution)/shard_map/all_to_all | solution.py:27
  61.4 26.2 %all-to-all-start.4 = ((bf16[32,2,1,1,3,2048]{5,1,4,3,2,0:T(2,128)(2,1)}), bf16[32,2,1,1,3,2048]{5,1,4,3,2,0:T(2,128)(2,1)S(1)}, u32[]{:S(2)}, u32[]{:S(2)}) async-start(bf16[32,2,1,1,3,2048]{5,1,4,3,2,0:T(2,128)(2,1)} %copy.65), calls=%async_computation.4 | async-start | bytes 1572864 | tf_op jit(solution)/shard_map/all_to_all | solution.py:27
  66.2 174.1 %all-gather.5.cloned.1.call-start = ((), (), s32[]{:S(2)}) async-start(), calls=%async_computation.10 | async-start | bytes 4423680 | tf_op jit(solution)/shard_map/all_gather | solution.py:68
  96.7 18.6 %copy-start.6 = (bf16[192,2048]{1,0:T(8,128)(2,1)S(1)}, bf16[192,2048]{1,0:T(8,128)(2,1)}, u32[]{:S(2)}) copy-start(bf16[192,2048]{1,0:T(8,128)(2,1)} %reshape_reshape_transpose_reshape.14) | copy-start | bytes 2359300
  118.5 0.7 copy-start.7
  128.2 30.6 %all-to-all-start.2 = ((bf16[32,2,1,1,3,2048]{5,1,4,3,2,0:T(2,128)(2,1)}), bf16[32,2,1,1,3,2048]{5,1,4,3,2,0:T(2,128)(2,1)S(1)}, u32[]{:S(2)}, u32[]{:S(2)}) async-start(bf16[32,2,1,1,3,2048]{5,1,4,3,2,0:T(2,128)(2,1)} %copy.62), calls=%async_computation.2 | async-start | bytes 1572864 | tf_op jit(solution)/shard_map/all_to_all | solution.py:27
  158.7 27.4 %all-to-all-start.8 = ((bf16[1,128,3,2048]{1,2,0,3:T(4,128)(2,1)}), bf16[1,128,3,2048]{1,2,0,3:T(4,128)(2,1)S(1)}, u32[]{:S(2)}, u32[]{:S(2)}) async-start(bf16[1,128,3,2048]{1,2,0,3:T(4,128)(2,1)} %copy.73), calls=%async_computation.8 | async-start | bytes 4194304 | tf_op jit(solution)/shard_map/all_to_all | solution.py:59
  196.0 30.9 %all-to-all-start.6 = ((bf16[32,2,1,1,3,2048]{5,1,4,3,2,0:T(2,128)(2,1)}), bf16[32,2,1,1,3,2048]{5,1,4,3,2,0:T(2,128)(2,1)}, u32[]{:S(2)}, u32[]{:S(2)}) async-start(bf16[32,2,1,1,3,2048]{5,1,4,3,2,0:T(2,128)(2,1)} %copy.68), calls=%async_computation.6 | async-start | bytes 1572864 | tf_op jit(solution)/shard_map/all_to_all | solution.py:27
  237.4 3.0 %copy-start.5 = (bf16[768,512]{1,0:T(8,128)(2,1)S(1)}, bf16[768,512]{1,0:T(8,128)(2,1)}, u32[]{:S(2)}) copy-start(bf16[768,512]{1,0:T(8,128)(2,1)} %reshape.53) | copy-start | bytes 2359300
  243.4 1.4 copy-start.4
  243.4 4.3 %copy-start.1 = (bf16[128,2048]{1,0:T(8,128)(2,1)S(1)}, bf16[128,2048]{1,0:T(8,128)(2,1)}, u32[]{:S(2)}) copy-start(bf16[128,2048]{1,0:T(8,128)(2,1)} %param.12) | copy-start | bytes 1572868
Sparse Core Ops, SparseCore 0:
  11.9 98.0 all-gather.2
  120.4 46.3 all-gather.4
where the time goes:
time: 256 us; the launch traced here: 255 us
  waiting for transfers between devices  82.2 us (32%)
  local copies, waits for them, and re-layouts  56.2 us (22%)
  starting transfers between devices  39.8 us (16%)
  blocking collectives  30.1 us (12%)
  matrix products  23.3 us (9%)
  between operations  14.4 us (6%)
  other arithmetic  8.59 us (3%)
    all_to_all x4, waiting for transfers between devices, turned_blocks(): lax.all_to_all(tiles, axes[k], split_axis=k, concat_axis=k, tiled=True)  58 us
    all_to_all x4, starting transfers between devices, turned_blocks(): lax.all_to_all(tiles, axes[k], split_axis=k, concat_axis=k, tiled=True)  35.9 us
    all_to_all x4, blocking collectives, turned_blocks(): lax.all_to_all(tiles, axes[k], split_axis=k, concat_axis=k, tiled=True)  30.1 us
    another operation x8, local copies, waits for them, and re-layouts, turned_blocks(): tiles = tiles.reshape(*lengths, *tiles.shape[1:])  15.4 us
    all_gather x1, waiting for transfers between devices, gather_turned(): filled = lax.all_gather(both, axis, axis=0, tiled=True)  13.3 us
    all_to_all x1, waiting for transfers between devices, sent_together(): lax.all_to_all(both, axis, split_axis=split_dim, concat_axis=concat_dim,...  10.9 us
    all_to_all x10, local copies, waits for them, and re-layouts, turned_blocks(): lax.all_to_all(tiles, axes[k], split_axis=k, concat_axis=k, tiled=True)  9.33 us
    dot_general x2, matrix products, contract_last(): lax.dot_general(left_side, right_side, (((1,), (1,)), ((), ())), preferre...  8.43 us
  transfers between devices with their start and end apart: 7, of which 6 were waited for; matrix products, arithmetic and copies ran while one was open for 26% of the time, Pallas kernels for 0%

commit v1 on v0

v1 whole, which is shorter than its diff:
```python
import functools

import jax
import jax.numpy as jnp
from jax import lax
from jax.experimental import pallas as pl
from jax.experimental.pallas import tpu as pltpu
from jax.sharding import Mesh
from jax.sharding import PartitionSpec as P

AXES = ("dp", "e_z", "e_x", "e_c")
EXPERT = ("e_z", "e_x", "e_c")
SLOTS = 3
MESH_ID = pl.DeviceIdType.MESH
BF16 = jnp.bfloat16
F32 = jnp.float32


def dot(a, b, dims=((1,), (0,))):
    return lax.dot_general(a, b, (dims, ((), ())), preferred_element_type=F32)


def layer_kernel(
    sizes,
    routes_ref, gate_ref, tok_ref, cot_ref, wg_ref, wu_ref, wd_ref,
    mixed_ref, gtok_ref, gwg_ref, gwu_ref, gwd_ref,
    xs, xb, xa, xc, gs, gb, ga, gc, ys, ya, yb, yc, ds, da, db, dc,
    perm, wgt, wut, wdt,
    gu_send, gu_recv, gu, gh_send, gh_recv, gh, hid, ggu,
    send_sem, recv_sem, dp_send, dp_recv,
):
    ny, nz, nx, nc = sizes
    na, nb = nz * nc, ny * nx
    tok_count, width = tok_ref.shape
    part = width // ny
    ff = wg_ref.shape[1]
    rows = na * nb * SLOTS
    own = rows // ny
    per = na // ny
    y, z, x, c = (lax.axis_index(a) for a in AXES)
    my_a = z * nc + c
    my_b = y * nx + x

    def dev_a(i):
        return (y, i // nc, x, lax.rem(i, nc))

    def dev_b(i):
        return (i // nx, z, lax.rem(i, nx), c)

    def dev_y(i):
        return (i, z, x, c)

    barrier = pltpu.get_barrier_semaphore()

    @pl.loop(1, na)
    def _(o):
        pl.semaphore_signal(barrier, inc=1, device_id=dev_a(lax.rem(my_a + o, na)), device_id_type=MESH_ID)

    @pl.loop(1, nb)
    def _(o):
        pl.semaphore_signal(barrier, inc=1, device_id=dev_b(lax.rem(my_b + o, nb)), device_id_type=MESH_ID)

    def copy_of(phase, src, dst, me, peer, o, dev):
        return pltpu.make_async_remote_copy(
            src_ref=src.at[peer], dst_ref=dst.at[me],
            send_sem=send_sem.at[phase, o], recv_sem=recv_sem.at[phase, me],
            device_id=dev(peer), device_id_type=MESH_ID,
        )

    def start_all(phase, src, dst, me, count, dev):
        @pl.loop(1, count)
        def _(o):
            copy_of(phase, src, dst, me, lax.rem(me + o, count), o, dev).start()
        dst[me] = src[me]

    def wait_recv(phase, src, dst, me, count, dev):
        @pl.loop(1, count)
        def _(o):
            s = lax.rem(me + o, count)
            pltpu.make_async_remote_copy(
                src_ref=src.at[s], dst_ref=dst.at[s],
                send_sem=send_sem.at[phase, o], recv_sem=recv_sem.at[phase, s],
                device_id=dev(s), device_id_type=MESH_ID,
            ).wait_recv()

    def wait_send(phase, src, dst, me, count, dev):
        @pl.loop(1, count)
        def _(o):
            copy_of(phase, src, dst, me, lax.rem(me + o, count), o, dev).wait_send()

    def dp_copy(kind, src, dst, o):
        return pltpu.make_async_remote_copy(
            src_ref=src, dst_ref=dst, send_sem=dp_send.at[kind, o], recv_sem=dp_recv.at[kind, o],
            device_id=dev_y(lax.rem(y + o, ny)), device_id_type=MESH_ID,
        )

    lane = lax.broadcasted_iota(jnp.int32, (tok_count, tok_count), 1)
    sub = lax.broadcasted_iota(jnp.int32, (tok_count, tok_count), 0)
    diag = lane == sub
    r_row = jnp.broadcast_to(routes_ref[...], (tok_count, tok_count))
    r_col = jnp.sum(jnp.where(diag, r_row, 0), axis=1, keepdims=True)
    same = r_row == r_col
    k_row = jnp.sum(jnp.where(same & (sub < lane), 1, 0), axis=0, keepdims=True)
    k_col = jnp.sum(jnp.where(same & (lane < sub), 1, 0), axis=1, keepdims=True)

    def place(r, k):
        rz, rx, rc = r // (nx * nc), lax.rem(r // nc, nx), lax.rem(r, nc)
        return rx * (na * SLOTS) + (rz * nc + rc) * SLOTS + k

    own_slots = nx * na * SLOTS
    base_row = place(routes_ref[...], k_row)
    base_col = place(r_col, k_col)
    pick_in = (lax.broadcasted_iota(jnp.int32, (own_slots, tok_count), 0) == base_row).astype(F32).astype(BF16)
    pick_out = (lax.broadcasted_iota(jnp.int32, (tok_count, own_slots), 1) == base_col).astype(F32).astype(BF16)
    weight = gate_ref[...].astype(F32) / 65536.0
    w_col = jnp.sum(jnp.where(diag, jnp.broadcast_to(weight, (tok_count, tok_count)), 0.0), axis=1, keepdims=True)

    for j in range(ny):
        cols = tok_ref[:, j * part:(j + 1) * part]
        xs[j * nx:(j + 1) * nx] = dot(pick_in, cols).astype(BF16).reshape(nx, na * SLOTS, part)

    pl.semaphore_wait(barrier, na + nb - 2)
    start_all(0, xs, xb, my_b, nb, dev_b)

    for j in range(ny):
        cols = (w_col * cot_ref[:, j * part:(j + 1) * part].astype(F32)).astype(BF16)
        gs[j * nx:(j + 1) * nx] = dot(pick_in, cols).astype(BF16).reshape(nx, na * SLOTS, part)

    start_all(1, gs, gb, my_b, nb, dev_b)

    n = lax.broadcasted_iota(jnp.int32, (rows, 128), 0)
    inner = lax.rem(n, na * SLOTS)
    source = (inner // SLOTS) * (nb * SLOTS) + (n // (na * SLOTS)) * SLOTS + lax.rem(inner, SLOTS)
    step = min(128, rows)
    for q in range(rows // step):
        at = lax.broadcasted_iota(jnp.int32, (rows, step), 1) + q * step
        perm[:, q * step:(q + 1) * step] = (at == source[:, :step]).astype(F32).astype(BF16)

    def turned(src, dst):
        @pl.loop(0, ny)
        def _(q):
            lines = perm[pl.ds(pl.multiple_of(q * own, own), own), :]
            dst[pl.ds(q * per, per)] = dot(lines, src[...].reshape(rows, part)).astype(BF16).reshape(per, nb * SLOTS, part)

    wgt[...] = wg_ref[...].T
    wut[...] = wu_ref[...].T
    wdt[...] = wd_ref[...].T

    wait_recv(0, xs, xb, my_b, nb, dev_b)
    turned(xb, xa)
    start_all(2, xa, xc, my_a, na, dev_a)

    wait_recv(1, gs, gb, my_b, nb, dev_b)
    turned(gb, ga)
    start_all(3, ga, gc, my_a, na, dev_a)

    def block(ref, q):
        return ref[pl.ds(q * per, per)].reshape(own, part)

    wait_recv(2, xa, xc, my_a, na, dev_a)

    @pl.loop(1, ny)
    def _(o):
        lines = block(xc, lax.rem(y + o, ny))
        gu_send[o - 1, :, :ff] = dot(lines, wg_ref[...]).astype(BF16)
        gu_send[o - 1, :, ff:] = dot(lines, wu_ref[...]).astype(BF16)
        dp_copy(0, gu_send.at[o - 1], gu_recv.at[o - 1], o).start()

    lines = block(xc, y)
    gu[:, :ff] = dot(lines, wg_ref[...])
    gu[:, ff:] = dot(lines, wu_ref[...])

    wait_recv(3, ga, gc, my_a, na, dev_a)

    @pl.loop(1, ny)
    def _(o):
        gh_send[o - 1] = dot(block(gc, lax.rem(y + o, ny)), wdt[...]).astype(BF16)
        dp_copy(1, gh_send.at[o - 1], gh_recv.at[o - 1], o).start()

    gh[...] = dot(block(gc, y), wdt[...])

    @pl.loop(1, ny)
    def _(o):
        dp_copy(0, gu_send.at[o - 1], gu_recv.at[o - 1], o).wait_recv()

    chunk = min(16, own)

    @pl.loop(0, own // chunk)
    def _(i):
        at = pl.ds(pl.multiple_of(i * chunk, chunk), chunk)
        total = gu[at, :]
        for o in range(ny - 1):
            total += gu_recv[o, at, :].astype(F32)
        gu[at, :] = total
        gate, up = total[:, :ff], total[:, ff:]
        hid[y, at, :] = (gate * jax.nn.sigmoid(gate) * up).astype(BF16)

    @pl.loop(1, ny)
    def _(o):
        dp_copy(2, hid.at[y], hid.at[y], o).start()

    @pl.loop(1, ny)
    def _(o):
        dp_copy(1, gh_send.at[o - 1], gh_recv.at[o - 1], o).wait_recv()

    @pl.loop(0, own // chunk)
    def _(i):
        at = pl.ds(pl.multiple_of(i * chunk, chunk), chunk)
        grad = gh[at, :]
        for o in range(ny - 1):
            grad += gh_recv[o, at, :].astype(F32)
        gate, up = gu[at, :ff], gu[at, ff:]
        s = jax.nn.sigmoid(gate)
        ggu[y, at, :ff] = (grad * up * s * (1.0 + gate * (1.0 - s))).astype(BF16)
        ggu[y, at, ff:] = (grad * gate * s).astype(BF16)

    @pl.loop(1, ny)
    def _(o):
        dp_copy(3, ggu.at[y], ggu.at[y], o).start()

    def down(q):
        ys[pl.ds(q * per, per)] = dot(hid[q], wd_ref[...]).astype(BF16).reshape(per, nb * SLOTS, part)

    def back(q):
        total = dot(ggu[q, :, :ff], wgt[...]) + dot(ggu[q, :, ff:], wut[...])
        ds[pl.ds(q * per, per)] = total.astype(BF16).reshape(per, nb * SLOTS, part)

    def from_dp(kind, buf, work):
        @pl.loop(0, ny)
        def _(o):
            q = lax.rem(y + ny - o, ny)

            @pl.when(o > 0)
            def _():
                dp_copy(kind, buf.at[q], buf.at[q], o).wait_recv()
            work(q)

    from_dp(2, hid, down)
    start_all(4, ys, ya, my_a, na, dev_a)
    from_dp(3, ggu, back)
    start_all(5, ds, da, my_a, na, dev_a)

    wait_recv(4, ys, ya, my_a, na, dev_a)
    turned(ya, yb)
    start_all(6, yb, yc, my_b, nb, dev_b)

    tn = ((0,), (0,))
    step = min(256, ff)
    for f in range(ff // step):
        cut = slice(f * step, (f + 1) * step)
        gwg_ref[:, cut] = dot(xc[...].reshape(rows, part), ggu[:, :, cut].reshape(rows, step), tn).astype(BF16)

    wait_recv(5, ds, da, my_a, na, dev_a)
    turned(da, db)
    start_all(7, db, dc, my_b, nb, dev_b)

    for f in range(ff // step):
        cut = slice(f * step, (f + 1) * step)
        high = slice(ff + f * step, ff + (f + 1) * step)
        gwu_ref[:, cut] = dot(xc[...].reshape(rows, part), ggu[:, :, high].reshape(rows, step), tn).astype(BF16)
        gwd_ref[cut, :] = dot(hid[:, :, cut].reshape(rows, step), gc[...].reshape(rows, part), tn).astype(BF16)

    wait_recv(6, yb, yc, my_b, nb, dev_b)
    for j in range(ny):
        picked = dot(pick_out, yc[j * nx:(j + 1) * nx].reshape(own_slots, part))
        mixed_ref[:, j * part:(j + 1) * part] = (w_col * picked).astype(BF16)

    wait_recv(7, db, dc, my_b, nb, dev_b)
    for j in range(ny):
        picked = dot(pick_out, dc[j * nx:(j + 1) * nx].reshape(own_slots, part))
        gtok_ref[:, j * part:(j + 1) * part] = picked.astype(BF16)

    wait_send(0, xs, xb, my_b, nb, dev_b)
    wait_send(1, gs, gb, my_b, nb, dev_b)
    wait_send(2, xa, xc, my_a, na, dev_a)
    wait_send(3, ga, gc, my_a, na, dev_a)
    wait_send(4, ys, ya, my_a, na, dev_a)
    wait_send(5, ds, da, my_a, na, dev_a)
    wait_send(6, yb, yc, my_b, nb, dev_b)
    wait_send(7, db, dc, my_b, nb, dev_b)

    @pl.loop(1, ny)
    def _(o):
        dp_copy(0, gu_send.at[o - 1], gu_recv.at[o - 1], o).wait_send()
        dp_copy(1, gh_send.at[o - 1], gh_recv.at[o - 1], o).wait_send()
        dp_copy(2, hid.at[y], hid.at[y], o).wait_send()
        dp_copy(3, ggu.at[y], ggu.at[y], o).wait_send()


def body(sizes, tokens, cotangent, routes, gate_fixed, w_gate, w_up, w_down):
    ny, nz, nx, nc = sizes
    na, nb = nz * nc, ny * nx
    tok_count, width = tokens.shape
    ff = w_gate.shape[2]
    part = width // ny
    rows = na * nb * SLOTS
    own = rows // ny
    by_b = pltpu.VMEM((nb, na * SLOTS, part), BF16)
    by_a = pltpu.VMEM((na, nb * SLOTS, part), BF16)
    vmem = pl.BlockSpec(memory_space=pltpu.VMEM)
    outs = pl.pallas_call(
        functools.partial(layer_kernel, sizes),
        out_shape=(
            jax.ShapeDtypeStruct((tok_count, width), BF16),
            jax.ShapeDtypeStruct((tok_count, width), BF16),
            jax.ShapeDtypeStruct((part, ff), BF16),
            jax.ShapeDtypeStruct((part, ff), BF16),
            jax.ShapeDtypeStruct((ff, part), BF16),
        ),
        in_specs=[vmem] * 7,
        out_specs=(vmem,) * 5,
        scratch_shapes=[
            by_b, by_b, by_a, by_a, by_b, by_b, by_a, by_a,
            by_a, by_a, by_b, by_b, by_a, by_a, by_b, by_b,
            pltpu.VMEM((rows, rows), BF16),
            pltpu.VMEM((ff, part), BF16),
            pltpu.VMEM((ff, part), BF16),
            pltpu.VMEM((part, ff), BF16),
            pltpu.VMEM((ny - 1, own, 2 * ff), BF16),
            pltpu.VMEM((ny - 1, own, 2 * ff), BF16),
            pltpu.VMEM((own, 2 * ff), F32),
            pltpu.VMEM((ny - 1, own, ff), BF16),
            pltpu.VMEM((ny - 1, own, ff), BF16),
            pltpu.VMEM((own, ff), F32),
            pltpu.VMEM((ny, own, ff), BF16),
            pltpu.VMEM((ny, own, 2 * ff), BF16),
            pltpu.SemaphoreType.DMA((8, max(na, nb))),
            pltpu.SemaphoreType.DMA((8, max(na, nb))),
            pltpu.SemaphoreType.DMA((4, ny)),
            pltpu.SemaphoreType.DMA((4, ny)),
        ],
        compiler_params=pltpu.CompilerParams(
            collective_id=0, has_side_effects=True, vmem_limit_bytes=60 * 2**20
        ),
    )(
        routes.reshape(1, tok_count), gate_fixed.reshape(1, tok_count), tokens, cotangent,
        w_gate[0], w_up[0], w_down[0],
    )
    mixed, grad_tokens, grad_w_gate, grad_w_up, grad_w_down = outs
    return mixed, grad_tokens, grad_w_gate[None], grad_w_up[None], grad_w_down[None]


def solution(mesh, split=(8, 4, 2)):
    sizes = (mesh.shape["dp"],) + split
    finer = Mesh(mesh.devices.reshape(sizes), AXES)
    tok = P(AXES, None)
    return jax.shard_map(
        functools.partial(body, sizes),
        mesh=finer,
        in_specs=(tok, tok, tok, tok, P(EXPERT, "dp", None), P(EXPERT, "dp", None), P(EXPERT, None, "dp")),
        out_specs=(tok, tok, P(EXPERT, "dp", None), P(EXPERT, "dp", None), P(EXPERT, None, "dp")),
        check_vma=False,
    )
```

time: 256 us -> 176 us (0.69)
  Pallas kernels: 0 us -> 167 us
  waiting for transfers between devices: 82.2 us -> 0 us
  local copies, waits for them, and re-layouts: 56.2 us -> 6.49 us
  starting transfers between devices: 39.8 us -> 0 us
  blocking collectives: 30.1 us -> 0 us
  matrix products: 23.3 us -> 0 us
  between operations: 14.4 us -> 0.66 us
  other arithmetic: 8.59 us -> 0 us
    pallas_call x0 -> x1, Pallas kernels: none -> 167 us  [body(): pl.pallas_call(functools.partial(layer_kernel, sizes), out_shape=(jax.Sha...]
    all_to_all x5 -> x0, waiting for transfers between devices: 68.9 us -> none  [the longest x4 58 us: turned_blocks(): lax.all_to_all(tiles, axes[k], split_axis=k, concat_axis=k, tiled=True)]
    all_to_all x5 -> x0, starting transfers between devices: 39.7 us -> none  [the longest x4 35.9 us: turned_blocks(): lax.all_to_all(tiles, axes[k], split_axis=k, concat_axis=k, tiled=True)]
    all_to_all x4 -> x0, blocking collectives: 30.1 us -> none  [turned_blocks(): lax.all_to_all(tiles, axes[k], split_axis=k, concat_axis=k, tiled=True)]
    another operation x14 -> x0, local copies, waits for them, and re-layouts: 23.8 us -> none  [the longest x8 15.4 us: turned_blocks(): tiles = tiles.reshape(*lengths, *tiles.shape[1:])]
    dot_general x6 -> x0, matrix products: 23.3 us -> none  [the longest x2 8.43 us: contract_last(): lax.dot_general(left_side, right_side, (((1,), (1,)), ((), ())), preferre...]
    all_gather x2 -> x0, waiting for transfers between devices: 13.3 us -> none  [the longest x1 13.3 us: gather_turned(): filled = lax.all_gather(both, axis, axis=0, tiled=True)]
    all_to_all x11 -> x0, local copies, waits for them, and re-layouts: 9.56 us -> none  [the longest x10 9.33 us: turned_blocks(): lax.all_to_all(tiles, axes[k], split_axis=k, concat_axis=k, tiled=True)]
  transfers between devices with their start and end apart: 7 -> 0, of which waited for: 6 -> 0; matrix products, arithmetic and copies ran while one was open for 26% -> 0% of each run, Pallas kernels for 0% -> 0%
where the time goes in v1:
time: 176 us; the launch traced here: 174 us
  Pallas kernels  167 us (95%)
  local copies, waits for them, and re-layouts  6.49 us (4%)
    pallas_call x1, Pallas kernels, body(): pl.pallas_call(functools.partial(layer_kernel, sizes), out_shape=(jax.Sha...  167 us
    unnamed x13, local copies, waits for them, and re-layouts  6.49 us

profile of v1, /device:TPU:1, one launch (start us, length us, event | category | flops | bytes accessed | tf_op | source)
XLA Modules:
  0.0 174.0 jit_solution(206754179406150387)
XLA Ops:
  0.6 166.8 %shard_map.110 = (bf16[128,2048]{1,0:T(8,128)(2,1)}, bf16[128,2048]{1,0:T(8,128)(2,1)}, bf16[512,768]{1,0:T(8,128)(2,1)}, bf16[512,768]{1,0:T(8,128)(2,1)}, bf16[768,512]{1,0:T(8,128)(2,1)}) custom-call(s32[1,128]{1,0:T(1,128)} %bitcast.14, s32[1,128]{1,0:T(1,128)} %bitcast.15, bf16[128,2048]{1,0:T(8,128)(2,1)} %tok_ref.1, bf16[128,2048]{1,0:T(8,128)(2,1)} %cot_ref.1, ...), custom_call_target="tpu_custom_call" | custom-call | tf_op jit(solution)/shard_map/pallas_call | solution.py:301
  167.5 0.0 copy-start.3
  167.5 0.0 copy-start.2
  167.5 2.0 %copy.17 = bf16[128,2048]{1,0:T(8,128)(2,1)} copy(bf16[128,2048]{1,0:T(8,128)(2,1)} %get-tuple-element.20) | data formatting | bytes 1048576
  169.5 0.0 copy-done.3
  169.5 0.8 copy.18
  170.3 0.0 copy-done.2
  170.3 0.0 copy-start.1
  170.3 0.9 copy.19
  171.1 0.5 copy-done.1
  171.7 0.0 copy-start
  171.7 0.9 copy.20
  172.6 0.5 copy-done
  173.1 0.9 copy.21
Async XLA Ops:
  167.5 2.0 %copy-start.3 = (bf16[128,2048]{1,0:T(8,128)(2,1)S(1)}, bf16[128,2048]{1,0:T(8,128)(2,1)}, u32[]{:S(2)}) copy-start(bf16[128,2048]{1,0:T(8,128)(2,1)} %get-tuple-element.21) | copy-start | bytes 1572868
  167.5 2.8 %copy-start.2 = (bf16[512,768]{1,0:T(8,128)(2,1)S(1)}, bf16[512,768]{1,0:T(8,128)(2,1)}, u32[]{:S(2)}) copy-start(bf16[512,768]{1,0:T(8,128)(2,1)} %get-tuple-element.12) | copy-start | bytes 2359300
  170.3 1.4 copy-start.1
  171.7 1.4 copy-start
